TPU v7x, 128 devices: a whole 4x4x4 slice. The times are simulated.
128 devices in a mesh: req: 32 (over y, z, core), tp: 4 (over x).
Axes of the slice: x: 4, y: 4, z: 4, core: 2. Of those that a mesh axis runs over, the one named last changes fastest.
Arguments:
- states: bfloat16 [64, 512, 1024], P('req', 'tp'), may hold values from -45 to 45
- lengths: int32 [64], P('req'), may hold values from 3 to 512, as said below
- w_qkv: bfloat16 [1024, 3, 1024], P(None, None, 'tp'), may hold values from -0.1875 to 0.1875
- b_qkv: float32 [3, 1024], P(None, 'tp'), may hold values from -3 to 3
- w_out: bfloat16 [1024, 1024], P('tp'), may hold values from -0.1875 to 0.1875
- b_out: float32 [1024], replicated, may hold values from -3 to 3
- ln1_gain: float32 [1024], replicated, may hold values from 0.1 to 1.9
- ln1_shift: float32 [1024], replicated, may hold values from -3 to 3
- w_up: bfloat16 [1024, 4096], P(None, 'tp'), may hold values from -0.1875 to 0.1875
- b_up: float32 [4096], P('tp'), may hold values from -3 to 3
- w_down: bfloat16 [4096, 1024], P('tp'), may hold values from -0.09375 to 0.09375
- b_down: float32 [1024], replicated, may hold values from -3 to 3
- ln2_gain: float32 [1024], replicated, may hold values from 0.1 to 1.9
- ln2_shift: float32 [1024], replicated, may hold values from -3 to 3
- index_rows: bfloat16 [524288, 1024], P(('req', 'tp')), may hold values from -0.1875 to 0.1875
- cand_ids: int32 [64, 64], P('req', 'tp'), may hold values from 0 to 524287
Outputs:
- hidden_out: bfloat16 [64, 512, 1024], P('req', 'tp')
- scores: float32 [64, 64], P('req', 'tp')
Inputs may be any that keep to these rules, and one draw needn't show every extreme that they name: Valid positions are the first lengths ones of a text; in every draw some text has 512.
All inputs are finite; a program needn't handle non-finite values.
Results may differ from a plain program's by a relative error of at most 0.015.
Values may be sent and summed in bfloat16 or wider, within the bound.
A program may use at most 128 MiB of HBM per device.

v0:
```python
import jax
import jax.numpy as jnp
from jax import lax
from jax.sharding import PartitionSpec as P

HEAD_DIM = 64
WINDOW = 512
layer_eps = 1e-05
norm_eps = 1e-06


def layer_norm(values, gain, shift):
    centre = values - jnp.mean(values, axis=-1, keepdims=True)
    spread = jnp.mean(centre * centre, axis=-1, keepdims=True)
    return centre * lax.rsqrt(spread + layer_eps) * gain + shift


def window_attention(queries_h, keys_h, values_h, length):
    seq_len = queries_h.shape[0]
    half_window = WINDOW // 2
    padding = ((half_window, half_window), (0, 0), (0, 0))
    keys_padded = jnp.pad(keys_h, padding)
    values_padded = jnp.pad(values_h, padding)
    scale_factor = HEAD_DIM ** (-0.5)

    def one_block(block_idx):
        blk_start = block_idx * WINDOW
        query_pos = blk_start + jnp.arange(WINDOW, dtype=jnp.int32)
        key_pos = blk_start - half_window + jnp.arange(2 * WINDOW, dtype=jnp.int32)
        keep_mask = (
            (jnp.abs(query_pos[:, None] - key_pos[None, :]) <= half_window)
            & (key_pos[None, :] >= 0)
            & (key_pos[None, :] < length)
        )
        logits = (
            jnp.einsum("qhe,khe->hqk", queries_h, keys_padded, preferred_element_type=jnp.float32)
            * scale_factor
        )
        logits = jnp.where(keep_mask[None], logits, jnp.float32(-1e30))
        top_val = jnp.max(logits, axis=-1, keepdims=True)
        expo = jnp.exp(logits - top_val)
        attn_weights = (expo / jnp.sum(expo, axis=-1, keepdims=True)).astype(jnp.bfloat16)
        context = jnp.einsum(
            "hqk,khe->qhe", attn_weights, values_padded, preferred_element_type=jnp.float32
        )
        context = jnp.where((query_pos < length)[:, None, None], context, jnp.float32(0.0))
        return context.astype(jnp.bfloat16)

    blocks = lax.map(one_block, jnp.arange(seq_len // WINDOW, dtype=jnp.int32))
    return blocks.reshape(seq_len, queries_h.shape[1] * HEAD_DIM)


def per_device(
    states,
    lengths,
    w_qkv,
    b_qkv,
    w_out,
    b_out,
    ln1_gain,
    ln1_shift,
    w_up,
    b_up,
    w_down,
    b_down,
    ln2_gain,
    ln2_shift,
    index_rows,
    cand_ids,
):
    tp_count = lax.axis_size("tp")
    tp_rank = lax.axis_index("tp")
    req_count = lax.axis_size("req")
    text_count, row_share, model_width = states.shape
    full_states = lax.all_gather(states, "tp", axis=1, tiled=True)
    seq_len = full_states.shape[1]
    local_width = w_qkv.shape[2]
    heads_here = local_width // HEAD_DIM
    projected = (
        jnp.einsum("tsd,dce->tsce", full_states, w_qkv, preferred_element_type=jnp.float32) + b_qkv
    ).astype(jnp.bfloat16)
    queries_h = projected[:, :, 0].reshape(text_count, seq_len, heads_here, HEAD_DIM)
    keys_h = projected[:, :, 1].reshape(text_count, seq_len, heads_here, HEAD_DIM)
    values_h = projected[:, :, 2].reshape(text_count, seq_len, heads_here, HEAD_DIM)

    def per_text(bundle):
        return window_attention(bundle[0], bundle[1], bundle[2], bundle[3])

    context = lax.map(per_text, (queries_h, keys_h, values_h, lengths))
    partial_value = jnp.einsum("tsk,kd->tsd", context, w_out, preferred_element_type=jnp.float32)
    attn_sum = lax.psum(partial_value.astype(jnp.bfloat16), "tp").astype(jnp.float32)
    normed_full = layer_norm(
        full_states.astype(jnp.float32) + attn_sum + b_out, ln1_gain, ln1_shift
    ).astype(jnp.bfloat16)
    normed_local = lax.dynamic_slice_in_dim(normed_full, tp_rank * row_share, row_share, 1)
    up_act = jax.nn.gelu(
        jnp.einsum("tsd,df->tsf", normed_full, w_up, preferred_element_type=jnp.float32) + b_up,
        approximate=False,
    ).astype(jnp.bfloat16)
    down_part = jnp.einsum("tsf,fd->tsd", up_act, w_down, preferred_element_type=jnp.float32)
    down_sum = lax.psum_scatter(
        down_part.astype(jnp.bfloat16), "tp", scatter_dimension=1, tiled=True
    ).astype(jnp.float32)
    hidden_out = layer_norm(
        normed_local.astype(jnp.float32) + down_sum + b_down, ln2_gain, ln2_shift
    ).astype(jnp.bfloat16)
    positions = tp_rank * row_share + jnp.arange(row_share, dtype=jnp.int32)
    is_valid = positions[None, :] < lengths[:, None]
    local_pool = jnp.sum(
        jnp.where(is_valid[:, :, None], hidden_out.astype(jnp.float32), jnp.float32(0.0)), axis=1
    )
    pooled = lax.psum(local_pool, "tp") / lengths.astype(jnp.float32)[:, None]
    query_vec = (
        pooled * lax.rsqrt(jnp.mean(pooled * pooled, axis=-1, keepdims=True) + norm_eps)
    ).astype(jnp.bfloat16)
    all_queries = lax.all_gather(query_vec, "req", axis=0, tiled=True)
    quarter = cand_ids.shape[1]
    gathered_ids = lax.all_gather(cand_ids, ("req", "tp"), axis=0, tiled=True)
    all_ids = (
        gathered_ids.reshape(req_count, tp_count, text_count, quarter)
        .transpose(0, 2, 1, 3)
        .reshape(req_count * text_count, tp_count * quarter)
    )
    rows_here = index_rows.shape[0]
    first_row = (lax.axis_index("req") * tp_count + tp_rank) * rows_here
    local_ids = all_ids - first_row
    is_owned = (local_ids >= 0) & (local_ids < rows_here)
    safe_ids = jnp.clip(local_ids, 0, rows_here - 1)
    fetched = jnp.take(index_rows, safe_ids.reshape(-1), axis=0).reshape(
        safe_ids.shape[0], safe_ids.shape[1], model_width
    )
    picked = jnp.einsum("td,tcd->tc", all_queries, fetched, preferred_element_type=jnp.float32)
    owner_terms = jnp.where(is_owned, picked, jnp.float32(0.0))
    owner_terms = (
        owner_terms.reshape(req_count, text_count, tp_count, quarter)
        .transpose(0, 2, 1, 3)
        .reshape(req_count * tp_count * text_count, quarter)
    )
    scores = lax.psum_scatter(owner_terms, ("req", "tp"), scatter_dimension=0, tiled=True)
    return (hidden_out, scores)


def solution(mesh):
    placed = (
        P("req", "tp", None),
        P("req"),
        P(None, None, "tp"),
        P(None, "tp"),
        P("tp", None),
        P(),
        P(),
        P(),
        P(None, "tp"),
        P("tp"),
        P("tp", None),
        P(),
        P(),
        P(),
        P(("req", "tp"), None),
        P("req", "tp"),
    )
    return jax.shard_map(
        per_device,
        mesh=mesh,
        in_specs=placed,
        out_specs=(P("req", "tp", None), P("req", "tp")),
        check_vma=False,
    )
```

profile of v0, /device:TPU:1, one launch (start us, length us, event | category | flops | bytes accessed | tf_op | source)
XLA Modules:
  0.0 362.5 jit_solution(10841223569805811967)
XLA Ops:
  7.2 0.7 all-gather.4.cloned.1.call-update
  8.0 35.7 %all-gather.4.cloned.1.call-done = bf16[2,512,1024]{2,1,0:T(8,128)(2,1)} async-done(((bf16[2,128,1024]{2,1,0:T(8,128)(2,1)}), bf16[2,512,1024]{2,1,0:T(8,128)(2,1)}) %all-gather.4.cloned.1.call-update) | async-done | bytes 2097168 | tf_op jit(solution)/shard_map/all_gather | solution.py:75
  43.7 3.9 %add_convert_fusion.1 = bf16[2,512,3,256]{1,3,2,0:T(8,128)(2,1)S(1)} fusion(f32[3,256]{1,0:T(4,128)} %param.21, bf16[1024,3,256]{2,0,1:T(8,128)(2,1)} %param.20, bf16[2,512,1024]{2,1,0:T(8,128)(2,1)} %all-gather.4.cloned.1.call-done), kind=kOutput, calls=%fused_computation.68 | convolution fusion | flops 1612185600 | bytes 5245952 | tf_op jit(solution)/shard_map/tsd,dce->tsce/dot_general | solution.py:80
  47.6 1.2 fusion.150
  48.8 33.0 %while.17 = (s32[]{:T(128)}, bf16[2,512,256]{1,2,0:T(8,128)(2,1)}, s32[2]{0:T(128)S(1)}, bf16[2,512,4,64]{1,3,2,0:T(8,128)(2,1)}, bf16[2,512,4,64]{1,3,2,0:T(8,1...) while((s32[]{:T(128)}, bf16[2,512,256]{1,2,0:T(8,128)(2,1)}, s32[2]{0:T(128)S(1)}, ...), condition=%wide.region_3.4_spmd, body=%wide.region_0.3_spmd.sunk | while | flops 552343040 | bytes 24671904 | solution.py:89
  49.5 0.7 fusion.164
  50.2 0.7 fusion.165
  50.9 1.1 dynamic-slice_bitcast_fusion.3
  52.0 6.9 %fusion.166 = (f32[4,512]{1,0:T(4,128)S(1)}, f32[4,512,1024]{2,1,0:T(8,128)}) fusion(pred[512,1024]{1,0:T(8,128)(4,1)S(1)} %fusion.165, bf16[512,4,64]{0,2,1:T(8,128)(2,1)S(1)} %get-tuple-element.195, bf16[2,512,4,64]{1,3,2,0:T(8,128)(2,1)} %get-tuple-element.217, s32[]{:T(128)} %get-tuple-element.206), kind=kOutput, calls=%fused_computation.171.clone.1 | convolution fusion | flops 276825088 | bytes 9445888 | tf_op jit(solution)/shard_map/while/body/eval_jaxpr/while/body/eval_jaxpr/sub | solution.py:41
  59.6 4.9 %fusion.167 = bf16[4,64,512]{2,1,0:T(8,128)(2,1)S(1)} fusion(f32[4,512,1024]{2,1,0:T(8,128)} %get-tuple-element.196, f32[4,512]{1,0:T(4,128)S(1)} %get-tuple-element.197, bf16[512,4,64]{0,2,1:T(8,128)(2,1)S(1)} %get-tuple-element.198, pred[512]{0:T(512)(128)(4,1)S(1)} %iota_compare_fusion.2), kind=kOutput, calls=%fused_computation.14.clone.1 | convolution fusion | flops 272891904 | bytes 8921600 | tf_op jit(solution)/shard_map/while/body/eval_jaxpr/while/body/eval_jaxpr/hqk,khe->qhe/dot_general | solution.py:43
  64.5 0.8 copy-done.5
  66.7 0.7 fusion.165
  67.4 1.1 dynamic-slice_bitcast_fusion.3
  68.5 6.9 %fusion.166 = (f32[4,512]{1,0:T(4,128)S(1)}, f32[4,512,1024]{2,1,0:T(8,128)}) fusion(pred[512,1024]{1,0:T(8,128)(4,1)S(1)} %fusion.165, bf16[512,4,64]{0,2,1:T(8,128)(2,1)S(1)} %get-tuple-element.195, bf16[2,512,4,64]{1,3,2,0:T(8,128)(2,1)} %get-tuple-element.217, s32[]{:T(128)} %get-tuple-element.206), kind=kOutput, calls=%fused_computation.171.clone.1 | convolution fusion | flops 276825088 | bytes 9445888 | tf_op jit(solution)/shard_map/while/body/eval_jaxpr/while/body/eval_jaxpr/sub | solution.py:41
  76.1 4.9 %fusion.167 = bf16[4,64,512]{2,1,0:T(8,128)(2,1)S(1)} fusion(f32[4,512,1024]{2,1,0:T(8,128)} %get-tuple-element.196, f32[4,512]{1,0:T(4,128)S(1)} %get-tuple-element.197, bf16[512,4,64]{0,2,1:T(8,128)(2,1)S(1)} %get-tuple-element.198, pred[512]{0:T(512)(128)(4,1)S(1)} %iota_compare_fusion.2), kind=kOutput, calls=%fused_computation.14.clone.1 | convolution fusion | flops 272891904 | bytes 8921600 | tf_op jit(solution)/shard_map/while/body/eval_jaxpr/while/body/eval_jaxpr/hqk,khe->qhe/dot_general | solution.py:43
  81.0 0.8 copy-done.5
  81.8 3.2 convolution_convert_fusion
  85.3 58.6 %all-reduce.5.cloned.1.call-done = bf16[2,512,1024]{2,1,0:T(8,128)(2,1)} async-done(((bf16[2,512,1024]{2,1,0:T(8,128)(2,1)}), bf16[2,512,1024]{2,1,0:T(8,128)(2,1)}) %all-reduce.5.cloned.1.call-update) | async-done | bytes 2097168 | tf_op jit(solution)/shard_map/psum | solution.py:91
  143.9 3.1 fusion.54
  147.4 1.1 multiply_reduce_fusion
  148.5 1.2 add_convert_fusion
  149.8 3.4 fusion.103
  153.2 12.5 %fusion.92 = bf16[2,512,1024]{2,1,0:T(8,128)(2,1)} fusion(bf16[1024,1024]{1,0:T(8,128)(2,1)S(1)} %copy-done.13, f32[2,512,1024]{2,1,0:T(8,128)S(1)} %get-tuple-element.149, f32[1024]{0:T(1024)S(1)} %copy-done.14, u8[512,1024]{1,0:T(8,128)(4,1)S(1)} %get-tuple-element.123, u8[512,1024]{1,0:T(8,128)(4,1)S(1)} %get-tuple-element.122), kind=kOutput, calls=%fused_computation.105 | convolution fusion | flops 2222981120 | bytes 9441280 | tf_op jit(solution)/shard_map/tsf,fd->tsd/dot_general | solution.py:100
  165.7 55.1 %all-gather = s32[128,2,16]{2,1,0:T(2,128)S(1)} all-gather(s32[1,2,16]{2,1,0:T(2,128)S(1)} %bitcast.89), channel_id=1, replica_groups=mesh['req'=32,'tp'=4] {'req','tp'}, dimensions={0}, use_global_device_ids=true | all-gather | bytes 16512 | tf_op jit(solution)/shard_map/all_gather | solution.py:118
  221.7 25.4 %gather_fusion = bf16[4096,1024]{1,0:T(8,128)(2,1)} fusion(bf16[4096,1024]{1,0:T(8,128)(2,1)} %param.32, s32[4096]{0:T(1024)S(1)} %broadcast_clamp_fusion), kind=kCustom, calls=%fused_computation | custom fusion | bytes 16793600 | tf_op jit(solution)/shard_map/jit(_take)/gather | solution.py:129
  247.2 1.5 fusion.104
  248.6 1.5 multiply_reduce_fusion.1
  250.2 2.4 select_reduce_fusion
  252.6 8.4 %psum.15 = f32[2,1024]{1,0:T(2,128)S(1)} all-reduce(f32[2,1024]{1,0:T(2,128)S(1)} %get-tuple-element.138), channel_id=1, replica_groups=mesh['req'=32,'tp'=4] {'tp'}, use_global_device_ids=true, to_apply=%region_11.12 | all-reduce | flops 2048 | bytes 16384 | tf_op jit(solution)/shard_map/psum | solution.py:112
  261.3 25.0 %all-gather.1 = bf16[32,2,1024]{2,1,0:T(2,128)(2,1)S(1)} all-gather(bf16[1,2,1024]{2,1,0:T(2,128)(2,1)S(1)} %fusion.108), channel_id=1, replica_groups=mesh['req'=32,'tp'=4] {'req'}, dimensions={0}, use_global_device_ids=true | all-gather | bytes 135168 | tf_op jit(solution)/shard_map/all_gather | solution.py:116
  286.4 4.7 %fusion.41 = f32[64,1,64]{2,1,0:T(1,128)S(1)} fusion(bf16[64,1024,1]{1,2,0:T(2,128)(2,1)S(1)} %reshape.275, bf16[64,64,1024]{2,1,0:T(8,128)(2,1)} %bitcast.75, pred[64,64]{1,0:T(8,128)(4,1)S(1)} %compare_and_fusion.1), kind=kOutput, calls=%fused_computation.38 | convolution fusion | flops 12582912 | bytes 8540160 | tf_op jit(solution)/shard_map/td,tcd->tc/dot_general | solution.py:132
  291.4 64.0 %all-reduce.2 = f32[256,16]{1,0:T(8,128)S(1)} all-reduce(f32[256,16]{1,0:T(8,128)S(1)} %bitcast.82), channel_id=3, replica_groups=mesh['req'=32,'tp'=4] {'req','tp'}, use_global_device_ids=true, to_apply=%region_13.14.clone | all-reduce | flops 4096 | bytes 32768
  (75 shorter events, 6.1 us)
Async XLA Ops:
  7.2 142.6 %copy-start = (bf16[1024,1024]{1,0:T(8,128)(2,1)S(1)}, bf16[1024,1024]{1,0:T(8,128)(2,1)}, u32[]{:S(2)}) copy-start(bf16[1024,1024]{1,0:T(8,128)(2,1)} %param.26) | copy-start | bytes 6291460
  7.2 36.5 %all-gather.4.cloned.1.call-start = ((), (), s32[]{:S(2)}) async-start(), calls=%async_computation.1 | async-start | bytes 2621440 | tf_op jit(solution)/shard_map/all_gather | solution.py:75
  7.9 136.0 %all-reduce.5.cloned.1.call-start = ((), (), s32[]{:S(2)}) async-start(), calls=%async_computation.2 | async-start | bytes 4194304 | tf_op jit(solution)/shard_map/psum | solution.py:91
  8.0 40.8 %copy-start.15 = (s32[2]{0:T(128)S(1)}, s32[2]{0:T(128)}, u32[]{:S(2)}) copy-start(s32[2]{0:T(128)} %param.19) | copy-start | bytes 28
  59.6 4.9 %copy-start.4 = (bf16[2,512,256]{1,2,0:T(8,128)(2,1)S(1)}, bf16[2,512,256]{1,2,0:T(8,128)(2,1)}, u32[]{:S(2)}) copy-start(bf16[2,512,256]{1,2,0:T(8,128)(2,1)} %get-tuple-element.207) | copy-start | bytes 1572868 | tf_op jit(solution)/shard_map/while
  64.5 0.8 copy-start.5
  76.0 4.9 %copy-start.4 = (bf16[2,512,256]{1,2,0:T(8,128)(2,1)S(1)}, bf16[2,512,256]{1,2,0:T(8,128)(2,1)}, u32[]{:S(2)}) copy-start(bf16[2,512,256]{1,2,0:T(8,128)(2,1)} %get-tuple-element.207) | copy-start | bytes 1572868 | tf_op jit(solution)/shard_map/while
  81.0 0.8 copy-start.5
  81.8 62.1 %copy-start.7 = (f32[1024]{0:T(1024)S(1)}, f32[1024]{0:T(1024)}, u32[]{:S(2)}) copy-start(f32[1024]{0:T(1024)} %param.23) | copy-start | bytes 12292
  85.1 63.4 %copy-start.10 = (f32[1024]{0:T(1024)S(1)}, f32[1024]{0:T(1024)}, u32[]{:S(2)}) copy-start(f32[1024]{0:T(1024)} %param.25) | copy-start | bytes 12292
  85.1 63.4 %copy-start.11 = (f32[1024]{0:T(1024)S(1)}, f32[1024]{0:T(1024)}, u32[]{:S(2)}) copy-start(f32[1024]{0:T(1024)} %param.24) | copy-start | bytes 12292
  85.1 162.1 %reduce-scatter.2.cloned.1.call-start = ((), (), s32[]{:S(2)}) async-start(), calls=%async_computation.3 | async-start | bytes 2621440 | tf_op jit(solution)/shard_map/reduce_scatter | solution.py:101
  143.9 3.1 copy-start.1
  143.9 3.5 copy-start.2
  148.4 1.3 copy-start.14
  149.8 3.4 copy-start.3
  149.8 3.4 copy-start.13
  153.2 12.5 %copy-start.12 = (s32[2,16]{1,0:T(2,128)S(1)}, s32[2,16]{1,0:T(2,128)}, u32[]{:S(2)}) copy-start(s32[2,16]{1,0:T(2,128)} %param.33) | copy-start | bytes 388
  221.6 25.5 %copy-start.6 = (f32[1024]{0:T(1024)S(1)}, f32[1024]{0:T(1024)}, u32[]{:S(2)}) copy-start(f32[1024]{0:T(1024)} %param.29) | copy-start | bytes 12292
  221.7 28.5 %copy-start.8 = (f32[1024]{0:T(1024)S(1)}, f32[1024]{0:T(1024)}, u32[]{:S(2)}) copy-start(f32[1024]{0:T(1024)} %param.31) | copy-start | bytes 12292
  221.7 28.5 %copy-start.9 = (f32[1024]{0:T(1024)S(1)}, f32[1024]{0:T(1024)}, u32[]{:S(2)}) copy-start(f32[1024]{0:T(1024)} %param.30) | copy-start | bytes 12292
Sparse Core Ops, SparseCore 0:
  9.7 34.0 all-gather.3
  85.2 58.6 all-reduce.4
  165.8 29.5 reduce-scatter.1
where the time goes:
time: 363 us
  blocking collectives  153 us (42%)
  waiting for transfers between devices  95 us (26%)
  matrix products  51.4 us (14%)
  local copies, waits for them, and re-layouts  33.3 us (9%)
  other arithmetic  15.6 us (4%)
  between operations  14.1 us (4%)
    unnamed x1, blocking collectives  64 us
    psum x1, waiting for transfers between devices, per_device(): lax.psum(partial_value.astype(jnp.bfloat16), 'tp').astype(jnp.float32)  58.6 us
    all_gather x1, blocking collectives, per_device(): gathered_ids = lax.all_gather(cand_ids, ('req', 'tp'), axis=0, tiled=True)  55.1 us
    all_gather x1, waiting for transfers between devices, per_device(): full_states = lax.all_gather(states, 'tp', axis=1, tiled=True)  35.7 us
    gather x1, local copies, waits for them, and re-layouts, per_device(): jnp.take(index_rows, safe_ids.reshape(-1), axis=0)  25.4 us
    all_gather x1, blocking collectives, per_device(): all_queries = lax.all_gather(query_vec, 'req', axis=0, tiled=True)  25 us
    sub x2, matrix products, one_block(): expo = jnp.exp(logits - top_val)  13.8 us
    dot_general x1, matrix products, per_device(): jnp.einsum('tsf,fd->tsd', up_act, w_down, preferred_element_type=jnp.floa...  12.5 us
  transfers between devices with their start and end apart: 3, of which 2 were waited for; matrix products, arithmetic and copies ran while one was open for 7% of the time, Pallas kernels for 0%

commit v1 on v0

--- a/solution.py
+++ b/solution.py
@@ -88,7 +88,9 @@
 
     context = lax.map(per_text, (queries_h, keys_h, values_h, lengths))
     partial_value = jnp.einsum("tsk,kd->tsd", context, w_out, preferred_element_type=jnp.float32)
-    attn_sum = lax.psum(partial_value.astype(jnp.bfloat16), "tp").astype(jnp.float32)
+    attn_sum = jnp.sum(lax.all_gather(partial_value.astype(jnp.bfloat16), "tp"), axis=0).astype(
+        jnp.float32
+    )
     normed_full = layer_norm(
         full_states.astype(jnp.float32) + attn_sum + b_out, ln1_gain, ln1_shift
     ).astype(jnp.bfloat16)

time: 363 us -> 395 us (1.088)
  waiting for transfers between devices: 95 us -> 120 us
  other arithmetic: 15.6 us -> 23 us
    all_gather x0 -> x1, waiting for transfers between devices: none -> 83.1 us  [per_device(): lax.all_gather(partial_value.astype(jnp.bfloat16), 'tp')]
    psum x1 -> x0, waiting for transfers between devices: 58.6 us -> none  [per_device(): lax.psum(partial_value.astype(jnp.bfloat16), 'tp').astype(jnp.float32)]
    reduce_sum x0 -> x1, other arithmetic: none -> 7.42 us  [per_device(): jnp.sum(lax.all_gather(partial_value.astype(jnp.bfloat16), 'tp'), axis=0)]
where the time goes in v1:
time: 395 us
  blocking collectives  153 us (39%)
  waiting for transfers between devices  120 us (30%)
  matrix products  51.3 us (13%)
  local copies, waits for them, and re-layouts  33.3 us (8%)
  other arithmetic  23 us (6%)
  between operations  14.1 us (4%)
    all_gather x1, waiting for transfers between devices, per_device(): lax.all_gather(partial_value.astype(jnp.bfloat16), 'tp')  83.1 us
    unnamed x1, blocking collectives  63.8 us
    all_gather x1, blocking collectives, per_device(): gathered_ids = lax.all_gather(cand_ids, ('req', 'tp'), axis=0, tiled=True)  56 us
    all_gather x1, waiting for transfers between devices, per_device(): full_states = lax.all_gather(states, 'tp', axis=1, tiled=True)  35.7 us
    all_gather x1, blocking collectives, per_device(): all_queries = lax.all_gather(query_vec, 'req', axis=0, tiled=True)  25.7 us
    gather x1, local copies, waits for them, and re-layouts, per_device(): jnp.take(index_rows, safe_ids.reshape(-1), axis=0)  25.4 us
    sub x2, matrix products, one_block(): expo = jnp.exp(logits - top_val)  13.8 us
    dot_general x1, matrix products, per_device(): jnp.einsum('tsf,fd->tsd', up_act, w_down, preferred_element_type=jnp.floa...  12.5 us
  transfers between devices with their start and end apart: 3, of which 2 were waited for; matrix products, arithmetic and copies ran while one was open for 7% of the time, Pallas kernels for 0%

profile of v1, /device:TPU:1, one launch (start us, length us, event | category | flops | bytes accessed | tf_op | source)
XLA Modules:
  0.0 394.6 jit_solution(3761492354183344975)
XLA Ops:
  7.2 0.7 all-gather.6.cloned.1.call-update
  8.0 35.7 %all-gather.6.cloned.1.call-done = bf16[2,512,1024]{2,1,0:T(8,128)(2,1)} async-done(((bf16[2,128,1024]{2,1,0:T(8,128)(2,1)}), bf16[2,512,1024]{2,1,0:T(8,128)(2,1)}) %all-gather.6.cloned.1.call-update) | async-done | bytes 2097168 | tf_op jit(solution)/shard_map/all_gather | solution.py:75
  43.7 3.9 add_convert_fusion.1
  47.6 1.2 fusion.150
  48.8 33.0 %while.17 = (s32[]{:T(128)}, bf16[2,512,256]{1,2,0:T(8,128)(2,1)}, s32[2]{0:T(128)S(1)}, bf16[2,512,4,64]{1,3,2,0:T(8,128)(2,1)}, bf16[2,512,4,64]{1,3,2,0:T(8,1...) while((s32[]{:T(128)}, bf16[2,512,256]{1,2,0:T(8,128)(2,1)}, s32[2]{0:T(128)S(1)}, ...), condition=%wide.region_3.4_spmd, body=%wide.region_0.3_spmd.sunk | while | flops 552343040 | bytes 24671904 | solution.py:89
  50.2 0.7 fusion.165
  50.9 1.1 dynamic-slice_bitcast_fusion.3
  52.0 6.9 %fusion.166 = (f32[4,512]{1,0:T(4,128)S(1)}, f32[4,512,1024]{2,1,0:T(8,128)}) fusion(pred[512,1024]{1,0:T(8,128)(4,1)S(1)} %fusion.165, bf16[512,4,64]{0,2,1:T(8,128)(2,1)S(1)} %get-tuple-element.195, bf16[2,512,4,64]{1,3,2,0:T(8,128)(2,1)} %get-tuple-element.217, s32[]{:T(128)} %get-tuple-element.206), kind=kOutput, calls=%fused_computation.171.clone.1 | convolution fusion | flops 276825088 | bytes 9445888 | tf_op jit(solution)/shard_map/while/body/eval_jaxpr/while/body/eval_jaxpr/sub | solution.py:41
  59.6 4.9 %fusion.167 = bf16[4,64,512]{2,1,0:T(8,128)(2,1)S(1)} fusion(f32[4,512,1024]{2,1,0:T(8,128)} %get-tuple-element.196, f32[4,512]{1,0:T(4,128)S(1)} %get-tuple-element.197, bf16[512,4,64]{0,2,1:T(8,128)(2,1)S(1)} %get-tuple-element.198, pred[512]{0:T(512)(128)(4,1)S(1)} %iota_compare_fusion.2), kind=kOutput, calls=%fused_computation.14.clone.1 | convolution fusion | flops 272891904 | bytes 8921600 | tf_op jit(solution)/shard_map/while/body/eval_jaxpr/while/body/eval_jaxpr/hqk,khe->qhe/dot_general | solution.py:43
  64.5 0.8 copy-done.5
  66.7 0.7 fusion.165
  67.4 1.1 dynamic-slice_bitcast_fusion.3
  68.5 6.9 %fusion.166 = (f32[4,512]{1,0:T(4,128)S(1)}, f32[4,512,1024]{2,1,0:T(8,128)}) fusion(pred[512,1024]{1,0:T(8,128)(4,1)S(1)} %fusion.165, bf16[512,4,64]{0,2,1:T(8,128)(2,1)S(1)} %get-tuple-element.195, bf16[2,512,4,64]{1,3,2,0:T(8,128)(2,1)} %get-tuple-element.217, s32[]{:T(128)} %get-tuple-element.206), kind=kOutput, calls=%fused_computation.171.clone.1 | convolution fusion | flops 276825088 | bytes 9445888 | tf_op jit(solution)/shard_map/while/body/eval_jaxpr/while/body/eval_jaxpr/sub | solution.py:41
  76.1 4.9 %fusion.167 = bf16[4,64,512]{2,1,0:T(8,128)(2,1)S(1)} fusion(f32[4,512,1024]{2,1,0:T(8,128)} %get-tuple-element.196, f32[4,512]{1,0:T(4,128)S(1)} %get-tuple-element.197, bf16[512,4,64]{0,2,1:T(8,128)(2,1)S(1)} %get-tuple-element.198, pred[512]{0:T(512)(128)(4,1)S(1)} %iota_compare_fusion.2), kind=kOutput, calls=%fused_computation.14.clone.1 | convolution fusion | flops 272891904 | bytes 8921600 | tf_op jit(solution)/shard_map/while/body/eval_jaxpr/while/body/eval_jaxpr/hqk,khe->qhe/dot_general | solution.py:43
  81.0 0.8 copy-done.5
  81.8 3.2 convolution_convert_fusion
  85.3 83.1 %all-gather.8.cloned.1.call-done = bf16[8,512,1024]{2,1,0:T(8,128)(2,1)} async-done(((bf16[2,512,1024]{2,1,0:T(8,128)(2,1)}), bf16[8,512,1024]{2,1,0:T(8,128)(2,1)}) %all-gather.8.cloned.1.call-update) | async-done | bytes 8388624 | tf_op jit(solution)/shard_map/all_gather | solution.py:91
  168.4 7.4 %reduce_sum.80 = bf16[2,512,1024]{2,1,0:T(8,128)(2,1)} reduce(bf16[4,2,512,1024]{3,2,1,0:T(8,128)(2,1)} %bitcast.77, bf16[]{:T(256)} %constant.156.clone.1), dimensions={0}, to_apply=%region_4.5 | reduce | flops 3145728 | bytes 10485762 | tf_op jit(solution)/shard_map/reduce_sum | solution.py:91
  175.8 3.1 fusion.54
  179.3 1.1 multiply_reduce_fusion
  180.4 1.2 add_convert_fusion
  181.7 3.4 fusion.103
  185.1 12.5 %fusion.92 = bf16[2,512,1024]{2,1,0:T(8,128)(2,1)} fusion(bf16[1024,1024]{1,0:T(8,128)(2,1)S(1)} %copy-done.13, f32[2,512,1024]{2,1,0:T(8,128)S(1)} %get-tuple-element.149, f32[1024]{0:T(1024)S(1)} %copy-done.14, u8[512,1024]{1,0:T(8,128)(4,1)S(1)} %get-tuple-element.123, u8[512,1024]{1,0:T(8,128)(4,1)S(1)} %get-tuple-element.122), kind=kOutput, calls=%fused_computation.105 | convolution fusion | flops 2222981120 | bytes 9441280 | tf_op jit(solution)/shard_map/tsf,fd->tsd/dot_general | solution.py:102
  197.6 56.0 %all-gather.1 = s32[128,2,16]{2,1,0:T(2,128)S(1)} all-gather(s32[1,2,16]{2,1,0:T(2,128)S(1)} %bitcast.91), channel_id=1, replica_groups=mesh['req'=32,'tp'=4] {'req','tp'}, dimensions={0}, use_global_device_ids=true | all-gather | bytes 16512 | tf_op jit(solution)/shard_map/all_gather | solution.py:120
  254.4 25.4 %gather_fusion = bf16[4096,1024]{1,0:T(8,128)(2,1)} fusion(bf16[4096,1024]{1,0:T(8,128)(2,1)} %param.32, s32[4096]{0:T(1024)S(1)} %broadcast_clamp_fusion), kind=kCustom, calls=%fused_computation | custom fusion | bytes 16793600 | tf_op jit(solution)/shard_map/jit(_take)/gather | solution.py:131
  279.9 1.5 fusion.104
  281.4 1.5 multiply_reduce_fusion.1
  283.0 2.4 select_reduce_fusion
  285.4 7.4 %psum.7 = f32[2,1024]{1,0:T(2,128)S(1)} all-reduce(f32[2,1024]{1,0:T(2,128)S(1)} %get-tuple-element.138), channel_id=1, replica_groups=mesh['req'=32,'tp'=4] {'tp'}, use_global_device_ids=true, to_apply=%region_11.12 | all-reduce | flops 2048 | bytes 16384 | tf_op jit(solution)/shard_map/psum | solution.py:114
  293.0 25.7 %all-gather.2 = bf16[32,2,1024]{2,1,0:T(2,128)(2,1)S(1)} all-gather(bf16[1,2,1024]{2,1,0:T(2,128)(2,1)S(1)} %fusion.108), channel_id=1, replica_groups=mesh['req'=32,'tp'=4] {'req'}, dimensions={0}, use_global_device_ids=true | all-gather | bytes 135168 | tf_op jit(solution)/shard_map/all_gather | solution.py:118
  318.8 4.7 %fusion.41 = f32[64,1,64]{2,1,0:T(1,128)S(1)} fusion(bf16[64,1024,1]{1,2,0:T(2,128)(2,1)S(1)} %reshape.276, bf16[64,64,1024]{2,1,0:T(8,128)(2,1)} %bitcast.76, pred[64,64]{1,0:T(8,128)(4,1)S(1)} %compare_and_fusion.1), kind=kOutput, calls=%fused_computation.38 | convolution fusion | flops 12582912 | bytes 8540160 | tf_op jit(solution)/shard_map/td,tcd->tc/dot_general | solution.py:134
  323.7 63.8 %all-reduce.2 = f32[256,16]{1,0:T(8,128)S(1)} all-reduce(f32[256,16]{1,0:T(8,128)S(1)} %bitcast.84), channel_id=4, replica_groups=mesh['req'=32,'tp'=4] {'req','tp'}, use_global_device_ids=true, to_apply=%region_13.14.clone | all-reduce | flops 4096 | bytes 32768
  (76 shorter events, 6.8 us)
Async XLA Ops:
  7.2 174.4 %copy-start = (bf16[1024,1024]{1,0:T(8,128)(2,1)S(1)}, bf16[1024,1024]{1,0:T(8,128)(2,1)}, u32[]{:S(2)}) copy-start(bf16[1024,1024]{1,0:T(8,128)(2,1)} %param.26) | copy-start | bytes 6291460
  7.2 36.5 %all-gather.6.cloned.1.call-start = ((), (), s32[]{:S(2)}) async-start(), calls=%async_computation.1 | async-start | bytes 2621440 | tf_op jit(solution)/shard_map/all_gather | solution.py:75
  7.9 160.4 %all-gather.8.cloned.1.call-start = ((), (), s32[]{:S(2)}) async-start(), calls=%async_computation.3 | async-start | bytes 10485760 | tf_op jit(solution)/shard_map/all_gather | solution.py:91
  8.0 40.8 %copy-start.15 = (s32[2]{0:T(128)S(1)}, s32[2]{0:T(128)}, u32[]{:S(2)}) copy-start(s32[2]{0:T(128)} %param.19) | copy-start | bytes 28
  59.6 4.9 %copy-start.4 = (bf16[2,512,256]{1,2,0:T(8,128)(2,1)S(1)}, bf16[2,512,256]{1,2,0:T(8,128)(2,1)}, u32[]{:S(2)}) copy-start(bf16[2,512,256]{1,2,0:T(8,128)(2,1)} %get-tuple-element.207) | copy-start | bytes 1572868 | tf_op jit(solution)/shard_map/while
  64.5 0.8 copy-start.5
  76.0 4.9 %copy-start.4 = (bf16[2,512,256]{1,2,0:T(8,128)(2,1)S(1)}, bf16[2,512,256]{1,2,0:T(8,128)(2,1)}, u32[]{:S(2)}) copy-start(bf16[2,512,256]{1,2,0:T(8,128)(2,1)} %get-tuple-element.207) | copy-start | bytes 1572868 | tf_op jit(solution)/shard_map/while
  81.0 0.8 copy-start.5
  85.1 194.8 %reduce-scatter.2.cloned.1.call-start = ((), (), s32[]{:S(2)}) async-start(), calls=%async_computation.2 | async-start | bytes 2621440 | tf_op jit(solution)/shard_map/reduce_scatter | solution.py:103
  168.4 7.4 %copy-start.7 = (f32[1024]{0:T(1024)S(1)}, f32[1024]{0:T(1024)}, u32[]{:S(2)}) copy-start(f32[1024]{0:T(1024)} %param.23) | copy-start | bytes 12292
  175.8 3.2 copy-start.1
  175.8 3.5 copy-start.2
  175.8 4.6 %copy-start.10 = (f32[1024]{0:T(1024)S(1)}, f32[1024]{0:T(1024)}, u32[]{:S(2)}) copy-start(f32[1024]{0:T(1024)} %param.25) | copy-start | bytes 12292
  175.8 4.6 %copy-start.11 = (f32[1024]{0:T(1024)S(1)}, f32[1024]{0:T(1024)}, u32[]{:S(2)}) copy-start(f32[1024]{0:T(1024)} %param.24) | copy-start | bytes 12292
  180.3 1.3 copy-start.14
  181.6 3.4 copy-start.3
  181.6 3.4 copy-start.13
  185.1 12.5 %copy-start.12 = (s32[2,16]{1,0:T(2,128)S(1)}, s32[2,16]{1,0:T(2,128)}, u32[]{:S(2)}) copy-start(s32[2,16]{1,0:T(2,128)} %param.33) | copy-start | bytes 388
  254.4 25.5 %copy-start.6 = (f32[1024]{0:T(1024)S(1)}, f32[1024]{0:T(1024)}, u32[]{:S(2)}) copy-start(f32[1024]{0:T(1024)} %param.29) | copy-start | bytes 12292
  254.4 28.5 %copy-start.8 = (f32[1024]{0:T(1024)S(1)}, f32[1024]{0:T(1024)}, u32[]{:S(2)}) copy-start(f32[1024]{0:T(1024)} %param.31) | copy-start | bytes 12292
  254.4 28.5 %copy-start.9 = (f32[1024]{0:T(1024)S(1)}, f32[1024]{0:T(1024)}, u32[]{:S(2)}) copy-start(f32[1024]{0:T(1024)} %param.30) | copy-start | bytes 12292
Sparse Core Ops, SparseCore 0:
  9.7 34.0 all-gather.5
  85.2 83.1 all-gather.7
  197.7 30.7 reduce-scatter.1
